TPU v7x, 256 devices: a whole 4x4x8 slice. The times are simulated.
256 devices in a mesh: tm: 8 (over x_hi, y), azim: 32 (over z, x_lo, core).
Axes of the slice: x: 4 (x_hi: 2, x_lo: 2; x = x_hi * 2 + x_lo), y: 4, z: 8, core: 2. Of those that a mesh axis runs over, the one named last changes fastest.
Arguments:
- rotor_coeffs: float32 [64, 2, 32, 16384], P('tm', None, 'azim'), may hold values from -1.5 to 1.5
- mortar_weights: float32 [64, 2, 32, 16384], P('tm', None, 'azim'), may hold values from 0.2 to 1
- block_shifts: int32 [64], P('tm'), may hold values from 0 to 31
- stencil_offsets: int32 [64, 2], P('tm'), may hold values from -1 to 1
- reluctivity: float32 [32, 16384], P('azim'), may hold values from 0.5 to 2
- source: float32 [64, 2, 32, 16384], P('tm', None, 'azim'), may hold values from -3 to 3
Outputs:
- residual: float32 [64, 2, 32, 16384], P('tm', None, 'azim')
All inputs are finite; a program needn't handle non-finite values.
Results may differ from a plain program's by a relative error of at most 0.0001.
Values sent between devices are 32-bit elements; how exact they have to be, the bound alone decides.
A program may use at most 128 MiB of HBM per device.

v0:
```python
import jax
import jax.numpy as jnp
from jax import lax
from jax.sharding import PartitionSpec as P

KC = 64
NT = 64


def shifted(value, axis, steps):
    count = lax.axis_size(axis)
    pairs = [(source, (source + steps) % count) for source in range(count)]
    return lax.ppermute(value, axis, pairs)


def with_halo(value, sides, width):
    for axis, dim in sides:
        devices, length = (lax.axis_size(axis), value.shape[dim])
        up = [(i, (i + 1) % devices) for i in range(devices)]
        down = [(j, i) for i, j in up]
        last = lax.slice_in_dim(value, length - width, length, axis=dim)
        initial = lax.slice_in_dim(value, 0, width, axis=dim)
        before = lax.ppermute(last, axis, up)
        after = lax.ppermute(initial, axis, down)
        value = jnp.concatenate([before, value, after], axis=dim)
    return value


def harmonic_basis(sample_rows, coefficient_count):
    column = jnp.arange(coefficient_count, dtype=jnp.int32)
    harmonic_order = 2 * (column // 2) + 1
    phase_index = harmonic_order[None, :] * (2 * sample_rows[:, None] + 1) % (4 * NT)
    phase_angle = phase_index.astype(jnp.float32) * (jnp.pi / (2 * NT))
    return jnp.where(column[None, :] % 2 == 0, jnp.cos(phase_angle), jnp.sin(phase_angle))


def body(rotor_coeffs, mortar_weights, block_shifts, stencil_offsets, reluctivity, source):
    sample_rows = mortar_weights.shape[0]
    stencil_count = mortar_weights.shape[1]
    full_table = harmonic_basis(jnp.arange(NT, dtype=jnp.int32), KC)
    spread = jnp.einsum(
        "jc,cabp->jabp",
        full_table,
        lax.all_to_all(rotor_coeffs, "tm", split_axis=3, concat_axis=0, tiled=True),
        precision=lax.Precision.HIGHEST,
    )
    samples = lax.all_to_all(spread, "tm", split_axis=0, concat_axis=3, tiled=True)
    turned = samples
    for bit_level in range((lax.axis_size("azim") - 1).bit_length()):
        moved = shifted(turned, "azim", 1 << bit_level)
        chosen = block_shifts >> bit_level & 1 == 1
        turned = jnp.where(chosen[:, None, None, None], moved, turned)
    padded = with_halo(turned, (("azim", 2),), 1)
    airgap_field = jnp.zeros_like(samples)
    for stencil_entry in range(stencil_count):
        pick_index = stencil_offsets[:, stencil_entry] + 1
        neighbour = jnp.zeros_like(samples)
        for position in range(3):
            neighbour = neighbour + jnp.where(
                (pick_index == position)[:, None, None, None],
                padded[:, :, position : position + 1],
                0.0,
            )
        airgap_field = airgap_field + mortar_weights[:, stencil_entry][:, None] * neighbour
    square = jnp.sum(airgap_field * airgap_field, axis=1, keepdims=True)
    field_flux = reluctivity[None, None] * (1.0 + square / (1.0 + square)) * airgap_field
    first_sample = lax.axis_index("tm") * sample_rows
    local_table = harmonic_basis(first_sample + jnp.arange(sample_rows, dtype=jnp.int32), KC) * (
        2.0 / NT
    )
    summed = lax.psum_scatter(
        jnp.einsum("jc,jabp->cabp", local_table, field_flux, precision=lax.Precision.HIGHEST),
        "tm",
        scatter_dimension=0,
        tiled=True,
    )
    return summed - source


def solution(mesh):
    in_specs = (
        P("tm", None, "azim", None),
        P("tm", None, "azim", None),
        P("tm"),
        P("tm", None),
        P("azim", None),
        P("tm", None, "azim", None),
    )
    out_specs = P("tm", None, "azim", None)
    return jax.shard_map(body, mesh=mesh, in_specs=in_specs, out_specs=out_specs, check_vma=False)
```

profile of v0, /device:TPU:1, one launch (start us, length us, event | category | flops | bytes accessed | tf_op | source)
XLA Modules:
  0.0 525.8 jit_solution(4220196497033002725)
XLA Ops:
  6.5 17.4 %copy.23 = f32[8,2,1,16384]{0,1,2,3:T(2,128)} copy(f32[8,2,1,16384]{3,2,1,0:T(1,128)} %param.6) | data formatting | bytes 2097152 | tf_op args[0]
  23.9 29.0 %reshape.168 = f32[8,1,32768]{2,1,0:T(1,128)} reshape(f32[16384,1,2,8]{3,2,1,0:T(2,128)} %bitcast.44) | data formatting | bytes 2097152
  52.9 7.5 %all-to-all-start = ((f32[8,1,32768]{2,1,0:T(1,128)}), f32[8,1,32768]{2,1,0:T(1,128)S(1)}, u32[]{:S(2)}, u32[]{:S(2)}) async-start(f32[8,1,32768]{2,1,0:T(1,128)} %reshape.168), calls=%async_computation | async-start | bytes 2097152 | tf_op jit(solution)/shard_map/all_to_all | solution.py:44
  60.4 0.2 reduce-scatter.2.cloned.1.call-start
  60.6 13.9 %all-to-all-done = f32[8,1,32768]{2,1,0:T(1,128)S(1)} async-done(((f32[8,1,32768]{2,1,0:T(1,128)}), f32[8,1,32768]{2,1,0:T(1,128)S(1)}, u32[]{:S(2)}, u32[]{:S(2)}) %all-to-all-start) | async-done | bytes 1048608 | tf_op jit(solution)/shard_map/all_to_all | solution.py:44
  74.5 0.5 broadcast.282
  75.0 3.1 reduce.1
  78.2 32.1 %reshape.169 = f32[16384,1,2,8]{3,2,1,0:T(2,128)} reshape(f32[8,32768]{1,0:T(8,128)S(1)} %reduce.1) | data formatting | bytes 2097152
  110.3 20.2 %copy.31 = f32[8,2,1,8,2048]{4,0,3,1,2:T(8,128)S(1)} copy(f32[8,2,1,8,2048]{0,1,4,3,2:T(2,128)} %bitcast.43) | data formatting | bytes 2097152 | tf_op jit(solution)/shard_map/all_to_all | solution.py:44
  130.5 0.0 copy-start.3
  130.5 0.0 copy-start.2
  130.5 1.3 convolution_bitcast_fusion.1
  131.8 0.8 copy.26
  132.6 21.4 %all_to_all.33 = f32[64,2,1,2048]{3,1,2,0:T(2,128)S(1)} all-to-all(f32[64,2,1,2048]{3,1,2,0:T(2,128)S(1)} %copy.26), channel_id=1, replica_groups=mesh['tm'=8,'azim'=32] {'tm'}, dimensions={0} | all-to-all | bytes 2097152 | tf_op jit(solution)/shard_map/all_to_all | solution.py:47
  154.0 0.6 copy.27
  154.6 2.8 collective-permute-start
  157.4 0.0 copy-done.4
  157.4 11.7 %collective-permute-done = f32[8,2,1,16384]{3,0,1,2:T(8,128)S(1)} collective-permute-done((f32[8,2,1,16384]{3,0,1,2:T(8,128)S(1)}, f32[8,2,1,16384]{3,0,1,2:T(8,128)S(1)}, u32[]{:S(2)}, u32[]{:S(2)}) %collective-permute-start) | collective-permute-done | bytes 1048608 | tf_op jit(solution)/shard_map/ppermute | solution.py:13
  169.2 0.2 broadcast_select_fusion
  169.3 2.5 collective-permute-start.1
  171.8 20.8 %collective-permute-done.1 = f32[8,2,1,16384]{3,0,1,2:T(8,128)S(1)} collective-permute-done((f32[8,2,1,16384]{3,0,1,2:T(8,128)S(1)}, f32[8,2,1,16384]{3,0,1,2:T(8,128)S(1)}, u32[]{:S(2)}, u32[]{:S(2)}) %collective-permute-start.1) | collective-permute-done | bytes 1048608 | tf_op jit(solution)/shard_map/ppermute | solution.py:13
  192.7 0.2 broadcast_select_fusion.1
  192.9 3.0 collective-permute-start.2
  195.9 21.3 %collective-permute-done.2 = f32[8,2,1,16384]{3,0,1,2:T(8,128)S(1)} collective-permute-done((f32[8,2,1,16384]{3,0,1,2:T(8,128)S(1)}, f32[8,2,1,16384]{3,0,1,2:T(8,128)S(1)}, u32[]{:S(2)}, u32[]{:S(2)}) %collective-permute-start.2) | collective-permute-done | bytes 1048608 | tf_op jit(solution)/shard_map/ppermute | solution.py:13
  217.2 0.2 broadcast_select_fusion.2
  217.3 5.8 %collective-permute-start.3 = (f32[8,2,1,16384]{3,0,1,2:T(8,128)S(1)}, f32[8,2,1,16384]{3,0,1,2:T(8,128)S(1)}, u32[]{:S(2)}, u32[]{:S(2)}) collective-permute-start(f32[8,2,1,16384]{3,0,1,2:T(8,128)S(1)} %broadcast_select_fusion.2), channel_id=1, source_target_pairs={{0,8},{1,9},{2,10},{3,11},{4,12},{5,13},{6,14},{7,15},{8,16},{9,17... | collective-permute-start | bytes 3145736 | tf_op jit(solution)/shard_map/ppermute | solution.py:13
  223.2 42.9 %collective-permute-done.3 = f32[8,2,1,16384]{3,0,1,2:T(8,128)S(1)} collective-permute-done((f32[8,2,1,16384]{3,0,1,2:T(8,128)S(1)}, f32[8,2,1,16384]{3,0,1,2:T(8,128)S(1)}, u32[]{:S(2)}, u32[]{:S(2)}) %collective-permute-start.3) | collective-permute-done | bytes 1048608 | tf_op jit(solution)/shard_map/ppermute | solution.py:13
  266.1 0.2 broadcast_select_fusion.3
  266.2 0.0 copy-start
  266.2 1.4 collective-permute-start.4
  267.7 0.0 copy-done.1
  267.7 0.1 fusion.56
  267.8 25.5 %collective-permute-done.4 = f32[8,2,1,16384]{3,0,1,2:T(8,128)S(1)} collective-permute-done((f32[8,2,1,16384]{3,0,1,2:T(8,128)S(1)}, f32[8,2,1,16384]{3,0,1,2:T(8,128)S(1)}, u32[]{:S(2)}, u32[]{:S(2)}) %collective-permute-start.4) | collective-permute-done | bytes 1048608 | tf_op jit(solution)/shard_map/ppermute | solution.py:13
  293.3 0.2 broadcast_select_fusion.4
  293.4 3.3 collective-permute-start.6
  296.7 3.6 collective-permute-start.5
  300.3 0.6 copy_bitcast_fusion
  300.9 0.0 copy-done.3
  301.0 11.8 %collective-permute-done.6 = f32[8,2,1,16384]{3,0,1,2:T(8,128)} collective-permute-done((f32[8,2,1,16384]{3,0,1,2:T(8,128)S(1)}, f32[8,2,1,16384]{3,0,1,2:T(8,128)}, u32[]{:S(2)}, u32[]{:S(2)}) %collective-permute-start.6) | collective-permute-done | bytes 1048608 | tf_op jit(solution)/shard_map/ppermute | solution.py:24
  312.8 0.0 collective-permute-done.5
  312.8 2.2 multiply_reduce_fusion
  315.0 0.0 copy-done.2
  315.0 0.1 fusion.4
  315.1 9.2 %convolution_bitcast_fusion = f32[64,2,1,16384]{3,0,1,2:T(8,128)} fusion(f32[8,2,1,16384]{3,0,1,2:T(8,128)S(1)} %get-tuple-element.6, f32[8,16384]{1,0:T(8,128)S(1)} %fusion.4, s32[8]{0:T(128)S(1)} %multiply_add_fusion.2, s32[64]{0:T(128)S(1)} %get-tuple-element.20, pred[64]{0:T(512)(128)(4,1)S(1)} %fusion.44), kind=kOutput, calls=%fused_computation | convolution fusion | flops 201596928 | bytes 9961824 | tf_op jit(solution)/shard_map/jc,jabp->cabp/dot_general | solution.py:72
  324.3 0.0 reduce-scatter.2.cloned.1.call-update
  324.3 190.7 %reduce-scatter.2.cloned.1.call-done = f32[8,2,1,16384]{3,0,1,2:T(8,128)} async-done(((f32[64,2,1,16384]{3,0,1,2:T(8,128)}), f32[8,2,1,16384]{3,0,1,2:T(8,128)}) %reduce-scatter.2.cloned.1.call-update) | async-done | bytes 1048592 | tf_op jit(solution)/shard_map/reduce_scatter | solution.py:71
  515.1 1.9 copy_subtract_fusion
  516.9 2.0 copy.29
  (8 shorter events, 0.0 us)
Async XLA Ops:
  52.9 21.7 %all-to-all-start = ((f32[8,1,32768]{2,1,0:T(1,128)}), f32[8,1,32768]{2,1,0:T(1,128)S(1)}, u32[]{:S(2)}, u32[]{:S(2)}) async-start(f32[8,1,32768]{2,1,0:T(1,128)} %reshape.168), calls=%async_computation | async-start | bytes 2097152 | tf_op jit(solution)/shard_map/all_to_all | solution.py:44
  60.4 454.7 %reduce-scatter.2.cloned.1.call-start = ((), (), s32[]{:S(2)}) async-start(), calls=%async_computation.3 | async-start | bytes 9437184 | tf_op jit(solution)/shard_map/reduce_scatter | solution.py:71
  110.3 47.1 %copy-start.4 = (s32[8]{0:T(128)S(1)}, s32[8]{0:T(128)}, u32[]{:S(2)}) copy-start(s32[8]{0:T(128)} %param.8) | copy-start | bytes 100
  110.3 157.4 %copy-start.1 = (f32[8,2,1,16384]{3,2,1,0:T(1,128)S(1)}, f32[8,2,1,16384]{3,2,1,0:T(1,128)}, u32[]{:S(2)}) copy-start(f32[8,2,1,16384]{3,2,1,0:T(1,128)} %param.7) | copy-start | bytes 3145732
  130.5 170.4 %copy-start.3 = (s32[8,2]{0,1:T(2,128)S(1)}, s32[8,2]{0,1:T(2,128)}, u32[]{:S(2)}) copy-start(s32[8,2]{0,1:T(2,128)} %param.9) | copy-start | bytes 196
  130.5 184.5 %copy-start.2 = (f32[1,16384]{1,0:T(1,128)S(1)}, f32[1,16384]{1,0:T(1,128)}, u32[]{:S(2)}) copy-start(f32[1,16384]{1,0:T(1,128)} %param.10) | copy-start | bytes 196612
  154.6 14.6 %collective-permute-start = (f32[8,2,1,16384]{3,0,1,2:T(8,128)S(1)}, f32[8,2,1,16384]{3,0,1,2:T(8,128)S(1)}, u32[]{:S(2)}, u32[]{:S(2)}) collective-permute-start(f32[8,2,1,16384]{3,0,1,2:T(8,128)S(1)} %bitcast.45), channel_id=1, source_target_pairs={{0,1},{1,2},{2,3},{3,4},{4,5},{5,6},{6,7},{7,8},{8,9},{9,10},{10,1... | collective-permute-start | bytes 3145736 | tf_op jit(solution)/shard_map/ppermute | solution.py:13
  169.3 23.3 %collective-permute-start.1 = (f32[8,2,1,16384]{3,0,1,2:T(8,128)S(1)}, f32[8,2,1,16384]{3,0,1,2:T(8,128)S(1)}, u32[]{:S(2)}, u32[]{:S(2)}) collective-permute-start(f32[8,2,1,16384]{3,0,1,2:T(8,128)S(1)} %broadcast_select_fusion), channel_id=1, source_target_pairs={{0,2},{1,3},{2,4},{3,5},{4,6},{5,7},{6,8},{7,9},{8,10},{9,11},{10,... | collective-permute-start | bytes 3145736 | tf_op jit(solution)/shard_map/ppermute | solution.py:13
  192.9 24.3 %collective-permute-start.2 = (f32[8,2,1,16384]{3,0,1,2:T(8,128)S(1)}, f32[8,2,1,16384]{3,0,1,2:T(8,128)S(1)}, u32[]{:S(2)}, u32[]{:S(2)}) collective-permute-start(f32[8,2,1,16384]{3,0,1,2:T(8,128)S(1)} %broadcast_select_fusion.1), channel_id=1, source_target_pairs={{0,4},{1,5},{2,6},{3,7},{4,8},{5,9},{6,10},{7,11},{8,12},{9,13},{1... | collective-permute-start | bytes 3145736 | tf_op jit(solution)/shard_map/ppermute | solution.py:13
  217.3 48.7 %collective-permute-start.3 = (f32[8,2,1,16384]{3,0,1,2:T(8,128)S(1)}, f32[8,2,1,16384]{3,0,1,2:T(8,128)S(1)}, u32[]{:S(2)}, u32[]{:S(2)}) collective-permute-start(f32[8,2,1,16384]{3,0,1,2:T(8,128)S(1)} %broadcast_select_fusion.2), channel_id=1, source_target_pairs={{0,8},{1,9},{2,10},{3,11},{4,12},{5,13},{6,14},{7,15},{8,16},{9,17... | collective-permute-start | bytes 3145736 | tf_op jit(solution)/shard_map/ppermute | solution.py:13
  266.2 248.8 %copy-start = (f32[8,2,1,16384]{3,2,1,0:T(1,128)S(1)}, f32[8,2,1,16384]{3,2,1,0:T(1,128)}, u32[]{:S(2)}) copy-start(f32[8,2,1,16384]{3,2,1,0:T(1,128)} %param.11) | copy-start | bytes 3145732
  266.2 27.0 %collective-permute-start.4 = (f32[8,2,1,16384]{3,0,1,2:T(8,128)S(1)}, f32[8,2,1,16384]{3,0,1,2:T(8,128)S(1)}, u32[]{:S(2)}, u32[]{:S(2)}) collective-permute-start(f32[8,2,1,16384]{3,0,1,2:T(8,128)S(1)} %broadcast_select_fusion.3), channel_id=1, source_target_pairs={{0,16},{1,17},{2,18},{3,19},{4,20},{5,21},{6,22},{7,23},{8,24},{9,... | collective-permute-start | bytes 3145736 | tf_op jit(solution)/shard_map/ppermute | solution.py:13
  293.4 19.4 %collective-permute-start.6 = (f32[8,2,1,16384]{3,0,1,2:T(8,128)S(1)}, f32[8,2,1,16384]{3,0,1,2:T(8,128)}, u32[]{:S(2)}, u32[]{:S(2)}) collective-permute-start(f32[8,2,1,16384]{3,0,1,2:T(8,128)S(1)} %broadcast_select_fusion.4), channel_id=1, source_target_pairs={{1,0},{2,1},{3,2},{4,3},{5,4},{6,5},{7,6},{8,7},{9,8},{10,9},{11,1... | collective-permute-start | bytes 3145736 | tf_op jit(solution)/shard_map/ppermute | solution.py:24
  296.7 16.1 %collective-permute-start.5 = (f32[8,2,1,16384]{3,0,1,2:T(8,128)S(1)}, f32[8,2,1,16384]{3,0,1,2:T(8,128)}, u32[]{:S(2)}, u32[]{:S(2)}) collective-permute-start(f32[8,2,1,16384]{3,0,1,2:T(8,128)S(1)} %broadcast_select_fusion.4), channel_id=1, source_target_pairs={{0,1},{1,2},{2,3},{3,4},{4,5},{5,6},{6,7},{7,8},{8,9},{9,10},{10,1... | collective-permute-start | bytes 3145736 | tf_op jit(solution)/shard_map/ppermute | solution.py:23
Sparse Core Ops, SparseCore 0:
  324.5 190.5 reduce-scatter.1
where the time goes:
time: 528 us; the launch traced here: 526 us
  waiting for transfers between devices  339 us (64%)
  local copies, waits for them, and re-layouts  103 us (20%)
  starting transfers between devices  30.2 us (6%)
  blocking collectives  21.4 us (4%)
  between operations  13.5 us (3%)
  matrix products  10.4 us (2%)
  other arithmetic  8.16 us (2%)
    reduce_scatter x1, waiting for transfers between devices, body(): lax.psum_scatter(jnp.einsum('jc,jabp->cabp', local_table, field_flux, pre...  191 us
    ppermute x5, waiting for transfers between devices, shifted(): return lax.ppermute(value, axis, pairs)  122 us
    unnamed x14, local copies, waits for them, and re-layouts  79.1 us
    all_to_all x1, blocking collectives, body(): lax.all_to_all(spread, 'tm', split_axis=0, concat_axis=3, tiled=True)  21.4 us
    all_to_all x2, local copies, waits for them, and re-layouts, body(): lax.all_to_all(rotor_coeffs, 'tm', split_axis=3, concat_axis=0, tiled=True)  20.7 us
    ppermute x5, starting transfers between devices, shifted(): return lax.ppermute(value, axis, pairs)  15.6 us
    all_to_all x1, waiting for transfers between devices, body(): lax.all_to_all(rotor_coeffs, 'tm', split_axis=3, concat_axis=0, tiled=True)  13.9 us
    ppermute x1, waiting for transfers between devices, with_halo(): after = lax.ppermute(initial, axis, down)  11.8 us
  transfers between devices with their start and end apart: 9, of which 8 were waited for; matrix products, arithmetic and copies ran while one was open for 0% of the time, Pallas kernels for 0%

commit v1 on v0

v1 whole, which is shorter than its diff:
```python
import jax
import jax.numpy as jnp
from jax import lax
from jax.sharding import PartitionSpec as P

KC = 64
NT = 64
LANES = 128


def shifted(value, axis, steps):
    count = lax.axis_size(axis)
    pairs = [(source, (source + steps) % count) for source in range(count)]
    return lax.ppermute(value, axis, pairs)


def harmonic_basis(sample_rows, coefficient_count):
    column = jnp.arange(coefficient_count, dtype=jnp.int32)
    harmonic_order = 2 * (column // 2) + 1
    phase_index = harmonic_order[None, :] * (2 * sample_rows[:, None] + 1) % (4 * NT)
    phase_angle = phase_index.astype(jnp.float32) * (jnp.pi / (2 * NT))
    return jnp.where(column[None, :] % 2 == 0, jnp.cos(phase_angle), jnp.sin(phase_angle))


def per_sample(flags, value):
    return flags.reshape((-1,) + (1,) * (value.ndim - 1))


def body(rotor_coeffs, mortar_weights, block_shifts, stencil_offsets, reluctivity, source):
    local_c, comp, _, nodes = rotor_coeffs.shape
    local_j, sten = mortar_weights.shape[:2]
    rows = nodes // LANES
    parts = lax.axis_size("tm")
    chunk = rows // parts
    coeffs = lax.all_to_all(
        rotor_coeffs.reshape(local_c, comp, rows, LANES), "tm", split_axis=2, concat_axis=0, tiled=True
    )
    weights = lax.all_to_all(
        mortar_weights.reshape(local_j, sten, rows, LANES), "tm", split_axis=2, concat_axis=0, tiled=True
    )
    shifts = lax.all_gather(block_shifts, "tm", tiled=True)
    offsets = lax.all_gather(stencil_offsets, "tm", tiled=True)
    gain = lax.dynamic_slice_in_dim(
        reluctivity.reshape(rows, LANES), lax.axis_index("tm") * chunk, chunk, axis=0
    )
    table = harmonic_basis(jnp.arange(NT, dtype=jnp.int32), KC)
    samples = jnp.einsum("jc,capk->japk", table, coeffs, precision=lax.Precision.HIGHEST)
    turned = samples
    for bit_level in range((lax.axis_size("azim") - 1).bit_length()):
        moved = shifted(turned, "azim", 1 << bit_level)
        chosen = (shifts >> bit_level) & 1 == 1
        turned = jnp.where(per_sample(chosen, turned), moved, turned)
    from_left = shifted(turned, "azim", 1)
    from_right = shifted(turned, "azim", -1)
    airgap_field = jnp.zeros_like(samples)
    for stencil_entry in range(sten):
        offset = offsets[:, stencil_entry]
        neighbour = jnp.where(
            per_sample(offset == 0, turned),
            turned,
            jnp.where(per_sample(offset > 0, turned), from_right, from_left),
        )
        airgap_field = airgap_field + weights[:, stencil_entry][:, None] * neighbour
    square = jnp.sum(airgap_field * airgap_field, axis=1, keepdims=True)
    field_flux = gain[None, None] * (1.0 + square / (1.0 + square)) * airgap_field
    summed = jnp.einsum(
        "jc,japk->capk", table * (2.0 / NT), field_flux, precision=lax.Precision.HIGHEST
    )
    residual = lax.all_to_all(summed, "tm", split_axis=0, concat_axis=2, tiled=True)
    return residual.reshape(source.shape) - source


def solution(mesh):
    in_specs = (
        P("tm", None, "azim", None),
        P("tm", None, "azim", None),
        P("tm"),
        P("tm", None),
        P("azim", None),
        P("tm", None, "azim", None),
    )
    out_specs = P("tm", None, "azim", None)
    return jax.shard_map(body, mesh=mesh, in_specs=in_specs, out_specs=out_specs, check_vma=False)
```

time: 528 us -> 304 us (0.58)
  the two profiles are of different devices: /device:TPU:1 before, /device:TPU:97 now
where the time goes in v1:
time: 304 us
  waiting for transfers between devices  121 us (40%)
  blocking collectives  110 us (36%)
  starting transfers between devices  51.1 us (17%)
  local copies, waits for them, and re-layouts  11 us (4%)
  other arithmetic  6.42 us (2%)
    ppermute x7, waiting for transfers between devices, shifted(): return lax.ppermute(value, axis, pairs)  107 us
    all_gather x1, blocking collectives, body(): offsets = lax.all_gather(stencil_offsets, 'tm', tiled=True)  52.3 us
    all_to_all x1, blocking collectives, body(): lax.all_to_all(summed, 'tm', split_axis=0, concat_axis=2, tiled=True)  46.4 us
    ppermute x7, starting transfers between devices, shifted(): return lax.ppermute(value, axis, pairs)  35.7 us
    all_to_all x1, waiting for transfers between devices, body(): lax.all_to_all(rotor_coeffs.reshape(local_c, comp, rows, LANES), 'tm', sp...  14.2 us
    unnamed x1, blocking collectives  11.8 us
    all_to_all x1, starting transfers between devices, body(): lax.all_to_all(mortar_weights.reshape(local_j, sten, rows, LANES), 'tm',...  8.69 us
    all_to_all x1, starting transfers between devices, body(): lax.all_to_all(rotor_coeffs.reshape(local_c, comp, rows, LANES), 'tm', sp...  6.65 us
  transfers between devices with their start and end apart: 9, of which 5 were waited for; matrix products, arithmetic and copies ran while one was open for 1% of the time, Pallas kernels for 0%

profile of v1, /device:TPU:97, one launch (start us, length us, event | category | flops | bytes accessed | tf_op | source)
XLA Modules:
  0.0 303.6 jit_solution(7695853863553865588)
XLA Ops:
  0.0 0.0 copy-start
  0.0 3.0 copy.28
  3.0 6.7 %all-to-all-start.1 = ((f32[8,2,128,128]{3,1,0,2:T(2,128)}), f32[8,2,128,128]{3,1,0,2:T(2,128)S(1)}, u32[]{:S(2)}, u32[]{:S(2)}) async-start(f32[8,2,128,128]{3,1,0,2:T(2,128)} %copy.28), calls=%async_computation.1 | async-start | bytes 2097152 | tf_op jit(solution)/shard_map/all_to_all | solution.py:35
  9.7 14.2 %all-to-all-done.1 = f32[8,2,128,128]{3,1,0,2:T(2,128)S(1)} async-done(((f32[8,2,128,128]{3,1,0,2:T(2,128)}), f32[8,2,128,128]{3,1,0,2:T(2,128)S(1)}, u32[]{:S(2)}, u32[]{:S(2)}) %all-to-all-start.1) | async-done | bytes 1048608 | tf_op jit(solution)/shard_map/all_to_all | solution.py:35
  23.9 0.3 copy.29
  24.2 1.8 fusion
  26.0 2.9 collective-permute-start
  28.9 0.7 copy-done.6
  29.6 0.6 dynamic-slice
  30.8 0.0 copy-start.5
  30.8 0.6 copy-done.5
  31.4 0.2 dynamic-update-slice
  31.6 11.8 %all-reduce = s32[64]{0:T(128)S(1)} all-reduce(s32[64]{0:T(128)S(1)} %dynamic-update-slice), channel_id=1, replica_groups=mesh['tm'=8,'azim'=32] {'tm'}, use_global_device_ids=true, to_apply=%add | all-reduce | flops 64 | bytes 512
  43.4 0.0 collective-permute-done
  43.4 0.2 broadcast_select_fusion
  43.7 1.0 collective-permute-start.1
  44.7 24.2 %collective-permute-done.1 = f32[64,2,16,128]{3,0,2,1:T(8,128)S(1)} collective-permute-done((f32[64,2,16,128]{3,0,2,1:T(8,128)S(1)}, f32[64,2,16,128]{3,0,2,1:T(8,128)S(1)}, u32[]{:S(2)}, u32[]{:S(2)}) %collective-permute-start.1) | collective-permute-done | bytes 1048608 | tf_op jit(solution)/shard_map/ppermute | solution.py:14
  68.9 0.2 broadcast_select_fusion.1
  69.2 3.4 %collective-permute-start.2 = (f32[64,2,16,128]{3,0,2,1:T(8,128)S(1)}, f32[64,2,16,128]{3,0,2,1:T(8,128)S(1)}, u32[]{:S(2)}, u32[]{:S(2)}) collective-permute-start(f32[64,2,16,128]{3,0,2,1:T(8,128)S(1)} %broadcast_select_fusion.1), channel_id=1, source_target_pairs={{0,4},{1,5},{2,6},{3,7},{4,8},{5,9},{6,10},{7,11},{8,12},{9,13},{1... | collective-permute-start | bytes 3145736 | tf_op jit(solution)/shard_map/ppermute | solution.py:14
  72.6 20.1 %collective-permute-done.2 = f32[64,2,16,128]{3,0,2,1:T(8,128)S(1)} collective-permute-done((f32[64,2,16,128]{3,0,2,1:T(8,128)S(1)}, f32[64,2,16,128]{3,0,2,1:T(8,128)S(1)}, u32[]{:S(2)}, u32[]{:S(2)}) %collective-permute-start.2) | collective-permute-done | bytes 1048608 | tf_op jit(solution)/shard_map/ppermute | solution.py:14
  92.7 0.2 broadcast_select_fusion.2
  93.0 2.8 collective-permute-start.3
  95.7 28.5 %collective-permute-done.3 = f32[64,2,16,128]{3,0,2,1:T(8,128)S(1)} collective-permute-done((f32[64,2,16,128]{3,0,2,1:T(8,128)S(1)}, f32[64,2,16,128]{3,0,2,1:T(8,128)S(1)}, u32[]{:S(2)}, u32[]{:S(2)}) %collective-permute-start.3) | collective-permute-done | bytes 1048608 | tf_op jit(solution)/shard_map/ppermute | solution.py:14
  124.2 0.2 broadcast_select_fusion.3
  124.5 5.7 %collective-permute-start.4 = (f32[64,2,16,128]{3,0,2,1:T(8,128)S(1)}, f32[64,2,16,128]{3,0,2,1:T(8,128)S(1)}, u32[]{:S(2)}, u32[]{:S(2)}) collective-permute-start(f32[64,2,16,128]{3,0,2,1:T(8,128)S(1)} %broadcast_select_fusion.3), channel_id=1, source_target_pairs={{0,16},{1,17},{2,18},{3,19},{4,20},{5,21},{6,22},{7,23},{8,24},{9,... | collective-permute-start | bytes 3145736 | tf_op jit(solution)/shard_map/ppermute | solution.py:14
  130.2 1.8 copy.24
  132.0 8.7 %all-to-all-start = ((f32[8,2,128,128]{3,1,0,2:T(2,128)}), f32[8,2,128,128]{3,1,0,2:T(2,128)S(1)}, u32[]{:S(2)}, u32[]{:S(2)}) async-start(f32[8,2,128,128]{3,1,0,2:T(2,128)} %copy.24), calls=%async_computation | async-start | bytes 2097152 | tf_op jit(solution)/shard_map/all_to_all | solution.py:38
  140.7 33.7 %collective-permute-done.4 = f32[64,2,16,128]{3,0,2,1:T(8,128)S(1)} collective-permute-done((f32[64,2,16,128]{3,0,2,1:T(8,128)S(1)}, f32[64,2,16,128]{3,0,2,1:T(8,128)S(1)}, u32[]{:S(2)}, u32[]{:S(2)}) %collective-permute-start.4) | collective-permute-done | bytes 1048608 | tf_op jit(solution)/shard_map/ppermute | solution.py:14
  174.4 1.0 copy-done.3
  175.4 1.4 broadcast_select_fusion.4
  176.8 20.0 %collective-permute-start.6 = (f32[64,2,16,128]{3,0,2,1:T(8,128)S(1)}, f32[64,2,16,128]{3,0,2,1:T(8,128)S(1)}, u32[]{:S(2)}, u32[]{:S(2)}) collective-permute-start(f32[64,2,16,128]{3,0,2,1:T(8,128)S(1)} %broadcast_select_fusion.4), channel_id=1, source_target_pairs={{0,1},{1,2},{2,3},{3,4},{4,5},{5,6},{6,7},{7,8},{8,9},{9,10},{10,1... | collective-permute-start | bytes 3145736 | tf_op jit(solution)/shard_map/ppermute | solution.py:14
  196.8 0.0 collective-permute-start.5
  196.8 0.7 copy-done.4
  197.4 52.3 %all-gather = s32[8,8,2]{1,2,0:T(2,128)S(1)} all-gather(s32[1,8,2]{1,2,0:T(2,128)S(1)} %bitcast.51), channel_id=1, replica_groups=mesh['tm'=8,'azim'=32] {'tm'}, dimensions={0}, use_global_device_ids=true | all-gather | bytes 576 | tf_op jit(solution)/shard_map/all_gather | solution.py:42
  249.8 0.1 reshape.115
  249.9 0.0 all-to-all-done
  249.9 0.1 copy.46
  250.0 0.1 slice_bitcast_fusion.1
  250.1 0.0 collective-permute-done.6
  250.1 0.0 collective-permute-done.5
  250.1 1.9 multiply_reduce_fusion
  252.0 0.1 fusion.6
  252.1 1.2 fusion.3
  253.3 0.6 copy.32
  254.0 46.4 %all_to_all.51 = f32[64,2,16,128]{3,2,1,0:T(8,128)S(1)} all-to-all(f32[64,2,16,128]{3,2,1,0:T(8,128)S(1)} %copy.32), channel_id=1, replica_groups=mesh['tm'=8,'azim'=32] {'tm'}, dimensions={0} | all-to-all | bytes 2097152 | tf_op jit(solution)/shard_map/all_to_all | solution.py:69
  300.3 0.1 copy.33
  300.4 1.1 copy-done.1
  301.5 2.1 sub.12
  (14 shorter events, 0.1 us)
Async XLA Ops:
  0.0 249.9 %copy-start = (f32[1,16384]{1,0:T(1,128)S(1)}, f32[1,16384]{1,0:T(1,128)}, u32[]{:S(2)}) copy-start(f32[1,16384]{1,0:T(1,128)} %param.10) | copy-start | bytes 196612
  3.0 20.8 %all-to-all-start.1 = ((f32[8,2,128,128]{3,1,0,2:T(2,128)}), f32[8,2,128,128]{3,1,0,2:T(2,128)S(1)}, u32[]{:S(2)}, u32[]{:S(2)}) async-start(f32[8,2,128,128]{3,1,0,2:T(2,128)} %copy.28), calls=%async_computation.1 | async-start | bytes 2097152 | tf_op jit(solution)/shard_map/all_to_all | solution.py:35
  26.0 17.4 %collective-permute-start = (f32[64,2,16,128]{3,0,2,1:T(8,128)S(1)}, f32[64,2,16,128]{3,0,2,1:T(8,128)S(1)}, u32[]{:S(2)}, u32[]{:S(2)}) collective-permute-start(f32[64,2,16,128]{3,0,2,1:T(8,128)S(1)} %fusion), channel_id=1, source_target_pairs={{0,1},{1,2},{2,3},{3,4},{4,5},{5,6},{6,7},{7,8},{8,9},{9,10},{10,1... | collective-permute-start | bytes 3145736 | tf_op jit(solution)/shard_map/ppermute | solution.py:14
  28.9 0.7 copy-start.6
  30.8 0.7 copy-start.5
  43.7 25.3 %collective-permute-start.1 = (f32[64,2,16,128]{3,0,2,1:T(8,128)S(1)}, f32[64,2,16,128]{3,0,2,1:T(8,128)S(1)}, u32[]{:S(2)}, u32[]{:S(2)}) collective-permute-start(f32[64,2,16,128]{3,0,2,1:T(8,128)S(1)} %broadcast_select_fusion), channel_id=1, source_target_pairs={{0,2},{1,3},{2,4},{3,5},{4,6},{5,7},{6,8},{7,9},{8,10},{9,11},{10,... | collective-permute-start | bytes 3145736 | tf_op jit(solution)/shard_map/ppermute | solution.py:14
  69.2 23.6 %collective-permute-start.2 = (f32[64,2,16,128]{3,0,2,1:T(8,128)S(1)}, f32[64,2,16,128]{3,0,2,1:T(8,128)S(1)}, u32[]{:S(2)}, u32[]{:S(2)}) collective-permute-start(f32[64,2,16,128]{3,0,2,1:T(8,128)S(1)} %broadcast_select_fusion.1), channel_id=1, source_target_pairs={{0,4},{1,5},{2,6},{3,7},{4,8},{5,9},{6,10},{7,11},{8,12},{9,13},{1... | collective-permute-start | bytes 3145736 | tf_op jit(solution)/shard_map/ppermute | solution.py:14
  93.0 31.3 %collective-permute-start.3 = (f32[64,2,16,128]{3,0,2,1:T(8,128)S(1)}, f32[64,2,16,128]{3,0,2,1:T(8,128)S(1)}, u32[]{:S(2)}, u32[]{:S(2)}) collective-permute-start(f32[64,2,16,128]{3,0,2,1:T(8,128)S(1)} %broadcast_select_fusion.2), channel_id=1, source_target_pairs={{0,8},{1,9},{2,10},{3,11},{4,12},{5,13},{6,14},{7,15},{8,16},{9,17... | collective-permute-start | bytes 3145736 | tf_op jit(solution)/shard_map/ppermute | solution.py:14
  124.2 5.9 %copy-start.2 = (f32[8,2,1,16384]{3,2,1,0:T(1,128)S(1)}, f32[8,2,1,16384]{3,2,1,0:T(1,128)}, u32[]{:S(2)}) copy-start(f32[8,2,1,16384]{3,2,1,0:T(1,128)} %param.7) | copy-start | bytes 3145732
  124.5 49.9 %collective-permute-start.4 = (f32[64,2,16,128]{3,0,2,1:T(8,128)S(1)}, f32[64,2,16,128]{3,0,2,1:T(8,128)S(1)}, u32[]{:S(2)}, u32[]{:S(2)}) collective-permute-start(f32[64,2,16,128]{3,0,2,1:T(8,128)S(1)} %broadcast_select_fusion.3), channel_id=1, source_target_pairs={{0,16},{1,17},{2,18},{3,19},{4,20},{5,21},{6,22},{7,23},{8,24},{9,... | collective-permute-start | bytes 3145736 | tf_op jit(solution)/shard_map/ppermute | solution.py:14
  132.0 117.9 %all-to-all-start = ((f32[8,2,128,128]{3,1,0,2:T(2,128)}), f32[8,2,128,128]{3,1,0,2:T(2,128)S(1)}, u32[]{:S(2)}, u32[]{:S(2)}) async-start(f32[8,2,128,128]{3,1,0,2:T(2,128)} %copy.24), calls=%async_computation | async-start | bytes 2097152 | tf_op jit(solution)/shard_map/all_to_all | solution.py:38
  174.4 1.0 copy-start.3
  176.8 73.3 %collective-permute-start.6 = (f32[64,2,16,128]{3,0,2,1:T(8,128)S(1)}, f32[64,2,16,128]{3,0,2,1:T(8,128)S(1)}, u32[]{:S(2)}, u32[]{:S(2)}) collective-permute-start(f32[64,2,16,128]{3,0,2,1:T(8,128)S(1)} %broadcast_select_fusion.4), channel_id=1, source_target_pairs={{0,1},{1,2},{2,3},{3,4},{4,5},{5,6},{6,7},{7,8},{8,9},{9,10},{10,1... | collective-permute-start | bytes 3145736 | tf_op jit(solution)/shard_map/ppermute | solution.py:14
  196.8 53.4 %collective-permute-start.5 = (f32[64,2,16,128]{3,0,2,1:T(8,128)S(1)}, f32[64,2,16,128]{3,0,2,1:T(8,128)}, u32[]{:S(2)}, u32[]{:S(2)}) collective-permute-start(f32[64,2,16,128]{3,0,2,1:T(8,128)S(1)} %broadcast_select_fusion.4), channel_id=1, source_target_pairs={{0,31},{1,0},{2,1},{3,2},{4,3},{5,4},{6,5},{7,6},{8,7},{9,8},{10,9... | collective-permute-start | bytes 3145736 | tf_op jit(solution)/shard_map/ppermute | solution.py:14
  196.8 0.7 copy-start.4
  300.3 1.2 copy-start.1

commit v2 on v1

--- a/solution.py
+++ b/solution.py
@@ -1,5 +1,8 @@
+import itertools
+
 import jax
 import jax.numpy as jnp
+import numpy as np
 from jax import lax
 from jax.sharding import PartitionSpec as P
 
@@ -26,6 +29,22 @@
     return flags.reshape((-1,) + (1,) * (value.ndim - 1))
 
 
+def digit_table(stages, count):
+    found = {}
+    for bits in itertools.product((0, 1), repeat=len(stages)):
+        found.setdefault(sum(b * s for b, s in zip(bits, stages)) % count, bits)
+    return np.array([found[d] for d in range(count)], np.int32)
+
+
+def barrel(value, amounts, stages, axis):
+    count = lax.axis_size(axis)
+    picks = jnp.take(jnp.asarray(digit_table(stages, count)), amounts % count, axis=0)
+    for level, steps in enumerate(stages):
+        moved = shifted(value, axis, steps)
+        value = jnp.where(per_sample(picks[:, level] == 1, value), moved, value)
+    return value
+
+
 def body(rotor_coeffs, mortar_weights, block_shifts, stencil_offsets, reluctivity, source):
     local_c, comp, _, nodes = rotor_coeffs.shape
     local_j, sten = mortar_weights.shape[:2]
@@ -38,29 +57,31 @@
     weights = lax.all_to_all(
         mortar_weights.reshape(local_j, sten, rows, LANES), "tm", split_axis=2, concat_axis=0, tiled=True
     )
-    shifts = lax.all_gather(block_shifts, "tm", tiled=True)
-    offsets = lax.all_gather(stencil_offsets, "tm", tiled=True)
+    small = jnp.concatenate([block_shifts[:, None], stencil_offsets], axis=1).astype(jnp.float32)
+    small = lax.all_gather(small, "tm", tiled=True).astype(jnp.int32)
+    shifts, offsets = small[:, 0], small[:, 1:]
     gain = lax.dynamic_slice_in_dim(
         reluctivity.reshape(rows, LANES), lax.axis_index("tm") * chunk, chunk, axis=0
     )
     table = harmonic_basis(jnp.arange(NT, dtype=jnp.int32), KC)
     samples = jnp.einsum("jc,capk->japk", table, coeffs, precision=lax.Precision.HIGHEST)
-    turned = samples
-    for bit_level in range((lax.axis_size("azim") - 1).bit_length()):
-        moved = shifted(turned, "azim", 1 << bit_level)
-        chosen = (shifts >> bit_level) & 1 == 1
-        turned = jnp.where(per_sample(chosen, turned), moved, turned)
-    from_left = shifted(turned, "azim", 1)
-    from_right = shifted(turned, "azim", -1)
-    airgap_field = jnp.zeros_like(samples)
-    for stencil_entry in range(sten):
-        offset = offsets[:, stencil_entry]
-        neighbour = jnp.where(
-            per_sample(offset == 0, turned),
-            turned,
-            jnp.where(per_sample(offset > 0, turned), from_right, from_left),
-        )
-        airgap_field = airgap_field + weights[:, stencil_entry][:, None] * neighbour
+    orders = ((1, 2, 4, -8, 16), (16, 8, -4, 2, 1))
+    fields = []
+    for component in range(comp):
+        turned = barrel(samples[:, component], shifts, orders[component % 2], "azim")
+        from_left = shifted(turned, "azim", 1)
+        from_right = shifted(turned, "azim", -1)
+        field = jnp.zeros_like(turned)
+        for stencil_entry in range(sten):
+            offset = offsets[:, stencil_entry]
+            neighbour = jnp.where(
+                per_sample(offset == 0, turned),
+                turned,
+                jnp.where(per_sample(offset > 0, turned), from_right, from_left),
+            )
+            field = field + weights[:, stencil_entry] * neighbour
+        fields.append(field)
+    airgap_field = jnp.stack(fields, axis=1)
     square = jnp.sum(airgap_field * airgap_field, axis=1, keepdims=True)
     field_flux = gain[None, None] * (1.0 + square / (1.0 + square)) * airgap_field
     summed = jnp.einsum(

time: 304 us -> 250 us (0.82)
  the two profiles are of different devices: /device:TPU:97 before, /device:TPU:1 now
where the time goes in v2:
time: 250 us
  starting transfers between devices  95.6 us (38%)
  waiting for transfers between devices  83.4 us (33%)
  blocking collectives  50.5 us (20%)
  local copies, waits for them, and re-layouts  10.1 us (4%)
  other arithmetic  6.77 us (3%)
  matrix products  2.96 us (1%)
    ppermute x14, starting transfers between devices, shifted(): return lax.ppermute(value, axis, pairs)  84.5 us
    ppermute x14, waiting for transfers between devices, shifted(): return lax.ppermute(value, axis, pairs)  78.3 us
    all_gather x1, blocking collectives, body(): small = lax.all_gather(small, 'tm', tiled=True).astype(jnp.int32)  34 us
    all_to_all x1, blocking collectives, body(): lax.all_to_all(summed, 'tm', split_axis=0, concat_axis=2, tiled=True)  16.5 us
    all_to_all x1, starting transfers between devices, body(): lax.all_to_all(rotor_coeffs.reshape(local_c, comp, rows, LANES), 'tm', sp...  7.48 us
    all_to_all x1, waiting for transfers between devices, body(): lax.all_to_all(mortar_weights.reshape(local_j, sten, rows, LANES), 'tm',...  5.02 us
  transfers between devices with their start and end apart: 16, of which 10 were waited for; matrix products, arithmetic and copies ran while one was open for 3% of the time, Pallas kernels for 0%

profile of v2, /device:TPU:1, one launch (start us, length us, event | category | flops | bytes accessed | tf_op | source)
XLA Modules:
  0.0 249.5 jit_solution(8012935296902372771)
XLA Ops:
  0.0 3.0 %copy.42 = f32[8,2,128,128]{3,1,0,2:T(2,128)} copy(f32[8,2,128,128]{3,2,1,0:T(8,128)} %bitcast.73) | data formatting | bytes 2097152 | tf_op jit(solution)/shard_map/reshape | solution.py:55
  3.0 7.5 %all-to-all-start.1 = ((f32[8,2,128,128]{3,1,0,2:T(2,128)}), f32[8,2,128,128]{3,1,0,2:T(2,128)S(1)}, u32[]{:S(2)}, u32[]{:S(2)}) async-start(f32[8,2,128,128]{3,1,0,2:T(2,128)} %copy.42), calls=%async_computation.1 | async-start | bytes 2097152 | tf_op jit(solution)/shard_map/all_to_all | solution.py:54
  10.5 0.7 copy-done.5
  11.2 34.0 %all-gather = f32[8,8,3]{1,2,0:T(4,128)S(1)} all-gather(f32[1,8,3]{1,2,0:T(4,128)S(1)} %fusion.25), channel_id=1, replica_groups=mesh['tm'=8,'azim'=32] {'tm'}, dimensions={0}, use_global_device_ids=true | all-gather | bytes 864 | tf_op jit(solution)/shard_map/all_gather | solution.py:61
  45.3 0.3 copy.43
  45.7 1.8 fusion
  47.6 5.6 %collective-permute-start = (f32[64,16,128]{2,0,1:T(8,128)S(1)}, f32[64,16,128]{2,0,1:T(8,128)S(1)}, u32[]{:S(2)}, u32[]{:S(2)}) collective-permute-start(f32[64,16,128]{2,0,1:T(8,128)S(1)} %get-tuple-element.22), channel_id=1, source_target_pairs={{0,1},{1,2},{2,3},{3,4},{4,5},{5,6},{6,7},{7,8},{8,9},{9,10},{10,1... | collective-permute-start | bytes 1572872 | tf_op jit(solution)/shard_map/ppermute | solution.py:17
  53.2 6.9 %collective-permute-start.7 = (f32[64,16,128]{2,0,1:T(8,128)S(1)}, f32[64,16,128]{2,0,1:T(8,128)S(1)}, u32[]{:S(2)}, u32[]{:S(2)}) collective-permute-start(f32[64,16,128]{2,0,1:T(8,128)S(1)} %get-tuple-element.23), channel_id=1, source_target_pairs={{0,16},{1,17},{2,18},{3,19},{4,20},{5,21},{6,22},{7,23},{8,24},{9,... | collective-permute-start | bytes 1572872 | tf_op jit(solution)/shard_map/ppermute | solution.py:17
  60.2 0.6 gather_fusion
  60.9 0.6 gather_fusion.1
  61.6 0.4 fusion.14
  62.0 12.7 %collective-permute-done.7 = f32[64,16,128]{2,0,1:T(8,128)S(1)} collective-permute-done((f32[64,16,128]{2,0,1:T(8,128)S(1)}, f32[64,16,128]{2,0,1:T(8,128)S(1)}, u32[]{:S(2)}, u32[]{:S(2)}) %collective-permute-start.7) | collective-permute-done | bytes 524320 | tf_op jit(solution)/shard_map/ppermute | solution.py:17
  74.7 0.2 broadcast_select_fusion.5
  74.9 7.1 %collective-permute-start.1 = (f32[64,16,128]{2,0,1:T(8,128)S(1)}, f32[64,16,128]{2,0,1:T(8,128)S(1)}, u32[]{:S(2)}, u32[]{:S(2)}) collective-permute-start(f32[64,16,128]{2,0,1:T(8,128)S(1)} %get-tuple-element.20), channel_id=1, source_target_pairs={{0,2},{1,3},{2,4},{3,5},{4,6},{5,7},{6,8},{7,9},{8,10},{9,11},{10,... | collective-permute-start | bytes 1572872 | tf_op jit(solution)/shard_map/ppermute | solution.py:17
  82.0 9.7 %collective-permute-start.8 = (f32[64,16,128]{2,0,1:T(8,128)S(1)}, f32[64,16,128]{2,0,1:T(8,128)S(1)}, u32[]{:S(2)}, u32[]{:S(2)}) collective-permute-start(f32[64,16,128]{2,0,1:T(8,128)S(1)} %get-tuple-element.21), channel_id=1, source_target_pairs={{0,8},{1,9},{2,10},{3,11},{4,12},{5,13},{6,14},{7,15},{8,16},{9,17... | collective-permute-start | bytes 1572872 | tf_op jit(solution)/shard_map/ppermute | solution.py:17
  91.7 8.9 %collective-permute-done.1 = f32[64,16,128]{2,0,1:T(8,128)S(1)} collective-permute-done((f32[64,16,128]{2,0,1:T(8,128)S(1)}, f32[64,16,128]{2,0,1:T(8,128)S(1)}, u32[]{:S(2)}, u32[]{:S(2)}) %collective-permute-start.1) | collective-permute-done | bytes 524320 | tf_op jit(solution)/shard_map/ppermute | solution.py:17
  100.6 0.1 broadcast_select_fusion.6
  100.7 1.0 collective-permute-start.2
  101.8 11.3 %collective-permute-done.8 = f32[64,16,128]{2,0,1:T(8,128)S(1)} collective-permute-done((f32[64,16,128]{2,0,1:T(8,128)S(1)}, f32[64,16,128]{2,0,1:T(8,128)S(1)}, u32[]{:S(2)}, u32[]{:S(2)}) %collective-permute-start.8) | collective-permute-done | bytes 524320 | tf_op jit(solution)/shard_map/ppermute | solution.py:17
  113.1 0.1 broadcast_select_fusion.1
  113.3 11.0 %collective-permute-done.2 = f32[64,16,128]{2,0,1:T(8,128)S(1)} collective-permute-done((f32[64,16,128]{2,0,1:T(8,128)S(1)}, f32[64,16,128]{2,0,1:T(8,128)S(1)}, u32[]{:S(2)}, u32[]{:S(2)}) %collective-permute-start.2) | collective-permute-done | bytes 524320 | tf_op jit(solution)/shard_map/ppermute | solution.py:17
  124.4 1.0 collective-permute-start.3
  125.4 1.0 collective-permute-done.9
  126.4 0.1 broadcast_select_fusion.2
  126.5 10.6 %collective-permute-start.10 = (f32[64,16,128]{2,0,1:T(8,128)S(1)}, f32[64,16,128]{2,0,1:T(8,128)S(1)}, u32[]{:S(2)}, u32[]{:S(2)}) collective-permute-start(f32[64,16,128]{2,0,1:T(8,128)S(1)} %broadcast_select_fusion.2), channel_id=1, source_target_pairs={{0,2},{1,3},{2,4},{3,5},{4,6},{5,7},{6,8},{7,9},{8,10},{9,11},{10,... | collective-permute-start | bytes 1572872 | tf_op jit(solution)/shard_map/ppermute | solution.py:17
  137.1 12.8 %collective-permute-done.3 = f32[64,16,128]{2,0,1:T(8,128)S(1)} collective-permute-done((f32[64,16,128]{2,0,1:T(8,128)S(1)}, f32[64,16,128]{2,0,1:T(8,128)S(1)}, u32[]{:S(2)}, u32[]{:S(2)}) %collective-permute-start.3) | collective-permute-done | bytes 524320 | tf_op jit(solution)/shard_map/ppermute | solution.py:17
  149.9 0.1 broadcast_select_fusion.8
  150.0 2.1 collective-permute-start.4
  152.3 26.2 %collective-permute-start.11 = (f32[64,16,128]{2,0,1:T(8,128)S(1)}, f32[64,16,128]{2,0,1:T(8,128)}, u32[]{:S(2)}, u32[]{:S(2)}) collective-permute-start(f32[64,16,128]{2,0,1:T(8,128)S(1)} %broadcast_select_fusion.3), channel_id=1, source_target_pairs={{0,1},{1,2},{2,3},{3,4},{4,5},{5,6},{6,7},{7,8},{8,9},{9,10},{10,1... | collective-permute-start | bytes 1572872 | tf_op jit(solution)/shard_map/ppermute | solution.py:17
  178.5 1.8 copy.37
  180.3 3.6 %all-to-all-start = ((f32[8,2,128,128]{3,1,0,2:T(2,128)}), f32[8,2,128,128]{3,1,0,2:T(2,128)S(1)}, u32[]{:S(2)}, u32[]{:S(2)}) async-start(f32[8,2,128,128]{3,1,0,2:T(2,128)} %copy.37), calls=%async_computation | async-start | bytes 2097152 | tf_op jit(solution)/shard_map/all_to_all | solution.py:57
  183.9 0.1 broadcast_select_fusion.9
  184.0 1.7 collective-permute-start.5
  185.7 7.0 %collective-permute-start.6 = (f32[64,16,128]{2,0,1:T(8,128)S(1)}, f32[64,16,128]{2,0,1:T(8,128)}, u32[]{:S(2)}, u32[]{:S(2)}) collective-permute-start(f32[64,16,128]{2,0,1:T(8,128)S(1)} %broadcast_select_fusion.9), channel_id=1, source_target_pairs={{0,1},{1,2},{2,3},{3,4},{4,5},{5,6},{6,7},{7,8},{8,9},{9,10},{10,1... | collective-permute-start | bytes 1572872 | tf_op jit(solution)/shard_map/ppermute | solution.py:17
  192.7 1.3 collective-permute-done.11
  194.0 1.2 broadcast_select_fusion.4
  195.1 5.5 %collective-permute-start.12 = (f32[64,16,128]{2,0,1:T(8,128)S(1)}, f32[64,16,128]{2,0,1:T(8,128)S(1)}, u32[]{:S(2)}, u32[]{:S(2)}) collective-permute-start(f32[64,16,128]{2,0,1:T(8,128)S(1)} %broadcast_select_fusion.4), channel_id=1, source_target_pairs={{0,31},{1,0},{2,1},{3,2},{4,3},{5,4},{6,5},{7,6},{8,7},{9,8},{10,9... | collective-permute-start | bytes 1572872 | tf_op jit(solution)/shard_map/ppermute | solution.py:17
  200.6 5.0 %all-to-all-done = f32[8,2,128,128]{3,1,0,2:T(2,128)S(1)} async-done(((f32[8,2,128,128]{3,1,0,2:T(2,128)}), f32[8,2,128,128]{3,1,0,2:T(2,128)S(1)}, u32[]{:S(2)}, u32[]{:S(2)}) %all-to-all-start) | async-done | bytes 1048608 | tf_op jit(solution)/shard_map/all_to_all | solution.py:57
  205.7 0.3 copy.38
  206.0 0.6 copy.61
  206.6 9.3 %collective-permute-done.5 = f32[64,16,128]{2,0,1:T(8,128)S(1)} collective-permute-done((f32[64,16,128]{2,0,1:T(8,128)S(1)}, f32[64,16,128]{2,0,1:T(8,128)S(1)}, u32[]{:S(2)}, u32[]{:S(2)}) %collective-permute-start.5) | collective-permute-done | bytes 524320 | tf_op jit(solution)/shard_map/ppermute | solution.py:17
  215.9 10.1 %collective-permute-done.12 = f32[64,16,128]{2,0,1:T(8,128)S(1)} collective-permute-done((f32[64,16,128]{2,0,1:T(8,128)S(1)}, f32[64,16,128]{2,0,1:T(8,128)S(1)}, u32[]{:S(2)}, u32[]{:S(2)}) %collective-permute-start.12) | collective-permute-done | bytes 524320 | tf_op jit(solution)/shard_map/ppermute | solution.py:17
  226.0 1.7 add_bitcast_fusion.1
  227.9 1.2 fusion.3
  229.2 0.6 copy.46
  229.8 16.5 %all_to_all.51 = f32[64,2,16,128]{3,2,1,0:T(8,128)S(1)} all-to-all(f32[64,2,16,128]{3,2,1,0:T(8,128)S(1)} %copy.46), channel_id=1, replica_groups=mesh['tm'=8,'azim'=32] {'tm'}, dimensions={0} | all-to-all | bytes 2097152 | tf_op jit(solution)/shard_map/all_to_all | solution.py:90
  246.3 1.1 copy-done.3
  247.5 2.1 sub.12
  (36 shorter events, 1.1 us)
Async XLA Ops:
  0.0 200.6 %copy-start = (f32[1,16384]{1,0:T(1,128)S(1)}, f32[1,16384]{1,0:T(1,128)}, u32[]{:S(2)}) copy-start(f32[1,16384]{1,0:T(1,128)} %param.14) | copy-start | bytes 196612
  3.0 42.3 %all-to-all-start.1 = ((f32[8,2,128,128]{3,1,0,2:T(2,128)}), f32[8,2,128,128]{3,1,0,2:T(2,128)S(1)}, u32[]{:S(2)}, u32[]{:S(2)}) async-start(f32[8,2,128,128]{3,1,0,2:T(2,128)} %copy.42), calls=%async_computation.1 | async-start | bytes 2097152 | tf_op jit(solution)/shard_map/all_to_all | solution.py:54
  10.5 0.7 copy-start.5
  10.5 0.7 copy-start.6
  47.5 12.7 %copy-start.1 = (s32[32,5]{1,0:T(8,128)S(1)}, s32[32,5]{1,0:T(8,128)}, u32[]{:S(2)}) copy-start(s32[32,5]{1,0:T(8,128)} %constant.99.clone2.1) | copy-start | bytes 1924
  47.6 14.4 %collective-permute-start = (f32[64,16,128]{2,0,1:T(8,128)S(1)}, f32[64,16,128]{2,0,1:T(8,128)S(1)}, u32[]{:S(2)}, u32[]{:S(2)}) collective-permute-start(f32[64,16,128]{2,0,1:T(8,128)S(1)} %get-tuple-element.22), channel_id=1, source_target_pairs={{0,1},{1,2},{2,3},{3,4},{4,5},{5,6},{6,7},{7,8},{8,9},{9,10},{10,1... | collective-permute-start | bytes 1572872 | tf_op jit(solution)/shard_map/ppermute | solution.py:17
  53.2 21.5 %collective-permute-start.7 = (f32[64,16,128]{2,0,1:T(8,128)S(1)}, f32[64,16,128]{2,0,1:T(8,128)S(1)}, u32[]{:S(2)}, u32[]{:S(2)}) collective-permute-start(f32[64,16,128]{2,0,1:T(8,128)S(1)} %get-tuple-element.23), channel_id=1, source_target_pairs={{0,16},{1,17},{2,18},{3,19},{4,20},{5,21},{6,22},{7,23},{8,24},{9,... | collective-permute-start | bytes 1572872 | tf_op jit(solution)/shard_map/ppermute | solution.py:17
  60.2 0.7 copy-start.2
  74.9 25.7 %collective-permute-start.1 = (f32[64,16,128]{2,0,1:T(8,128)S(1)}, f32[64,16,128]{2,0,1:T(8,128)S(1)}, u32[]{:S(2)}, u32[]{:S(2)}) collective-permute-start(f32[64,16,128]{2,0,1:T(8,128)S(1)} %get-tuple-element.20), channel_id=1, source_target_pairs={{0,2},{1,3},{2,4},{3,5},{4,6},{5,7},{6,8},{7,9},{8,10},{9,11},{10,... | collective-permute-start | bytes 1572872 | tf_op jit(solution)/shard_map/ppermute | solution.py:17
  82.0 31.1 %collective-permute-start.8 = (f32[64,16,128]{2,0,1:T(8,128)S(1)}, f32[64,16,128]{2,0,1:T(8,128)S(1)}, u32[]{:S(2)}, u32[]{:S(2)}) collective-permute-start(f32[64,16,128]{2,0,1:T(8,128)S(1)} %get-tuple-element.21), channel_id=1, source_target_pairs={{0,8},{1,9},{2,10},{3,11},{4,12},{5,13},{6,14},{7,15},{8,16},{9,17... | collective-permute-start | bytes 1572872 | tf_op jit(solution)/shard_map/ppermute | solution.py:17
  100.7 23.6 %collective-permute-start.2 = (f32[64,16,128]{2,0,1:T(8,128)S(1)}, f32[64,16,128]{2,0,1:T(8,128)S(1)}, u32[]{:S(2)}, u32[]{:S(2)}) collective-permute-start(f32[64,16,128]{2,0,1:T(8,128)S(1)} %broadcast_select_fusion.6), channel_id=1, source_target_pairs={{0,4},{1,5},{2,6},{3,7},{4,8},{5,9},{6,10},{7,11},{8,12},{9,13},{1... | collective-permute-start | bytes 1572872 | tf_op jit(solution)/shard_map/ppermute | solution.py:17
  113.2 13.1 %collective-permute-start.9 = (f32[64,16,128]{2,0,1:T(8,128)S(1)}, f32[64,16,128]{2,0,1:T(8,128)S(1)}, u32[]{:S(2)}, u32[]{:S(2)}) collective-permute-start(f32[64,16,128]{2,0,1:T(8,128)S(1)} %broadcast_select_fusion.1), channel_id=1, source_target_pairs={{0,28},{1,29},{2,30},{3,31},{4,0},{5,1},{6,2},{7,3},{8,4},{9,5},{1... | collective-permute-start | bytes 1572872 | tf_op jit(solution)/shard_map/ppermute | solution.py:17
  124.4 25.5 %collective-permute-start.3 = (f32[64,16,128]{2,0,1:T(8,128)S(1)}, f32[64,16,128]{2,0,1:T(8,128)S(1)}, u32[]{:S(2)}, u32[]{:S(2)}) collective-permute-start(f32[64,16,128]{2,0,1:T(8,128)S(1)} %broadcast_select_fusion.7), channel_id=1, source_target_pairs={{0,24},{1,25},{2,26},{3,27},{4,28},{5,29},{6,30},{7,31},{8,0},{9,1... | collective-permute-start | bytes 1572872 | tf_op jit(solution)/shard_map/ppermute | solution.py:17
  126.5 25.6 %collective-permute-start.10 = (f32[64,16,128]{2,0,1:T(8,128)S(1)}, f32[64,16,128]{2,0,1:T(8,128)S(1)}, u32[]{:S(2)}, u32[]{:S(2)}) collective-permute-start(f32[64,16,128]{2,0,1:T(8,128)S(1)} %broadcast_select_fusion.2), channel_id=1, source_target_pairs={{0,2},{1,3},{2,4},{3,5},{4,6},{5,7},{6,8},{7,9},{8,10},{9,11},{10,... | collective-permute-start | bytes 1572872 | tf_op jit(solution)/shard_map/ppermute | solution.py:17
  150.0 28.5 %copy-start.4 = (f32[8,2,1,16384]{3,2,1,0:T(1,128)S(1)}, f32[8,2,1,16384]{3,2,1,0:T(1,128)}, u32[]{:S(2)}) copy-start(f32[8,2,1,16384]{3,2,1,0:T(1,128)} %param.11) | copy-start | bytes 3145732
  150.0 33.8 %collective-permute-start.4 = (f32[64,16,128]{2,0,1:T(8,128)S(1)}, f32[64,16,128]{2,0,1:T(8,128)S(1)}, u32[]{:S(2)}, u32[]{:S(2)}) collective-permute-start(f32[64,16,128]{2,0,1:T(8,128)S(1)} %broadcast_select_fusion.8), channel_id=1, source_target_pairs={{0,16},{1,17},{2,18},{3,19},{4,20},{5,21},{6,22},{7,23},{8,24},{9,... | collective-permute-start | bytes 1572872 | tf_op jit(solution)/shard_map/ppermute | solution.py:17
  152.3 41.7 %collective-permute-start.11 = (f32[64,16,128]{2,0,1:T(8,128)S(1)}, f32[64,16,128]{2,0,1:T(8,128)}, u32[]{:S(2)}, u32[]{:S(2)}) collective-permute-start(f32[64,16,128]{2,0,1:T(8,128)S(1)} %broadcast_select_fusion.3), channel_id=1, source_target_pairs={{0,1},{1,2},{2,3},{3,4},{4,5},{5,6},{6,7},{7,8},{8,9},{9,10},{10,1... | collective-permute-start | bytes 1572872 | tf_op jit(solution)/shard_map/ppermute | solution.py:17
  180.3 25.4 %all-to-all-start = ((f32[8,2,128,128]{3,1,0,2:T(2,128)}), f32[8,2,128,128]{3,1,0,2:T(2,128)S(1)}, u32[]{:S(2)}, u32[]{:S(2)}) async-start(f32[8,2,128,128]{3,1,0,2:T(2,128)} %copy.37), calls=%async_computation | async-start | bytes 2097152 | tf_op jit(solution)/shard_map/all_to_all | solution.py:57
  184.0 31.9 %collective-permute-start.5 = (f32[64,16,128]{2,0,1:T(8,128)S(1)}, f32[64,16,128]{2,0,1:T(8,128)S(1)}, u32[]{:S(2)}, u32[]{:S(2)}) collective-permute-start(f32[64,16,128]{2,0,1:T(8,128)S(1)} %broadcast_select_fusion.9), channel_id=1, source_target_pairs={{0,31},{1,0},{2,1},{3,2},{4,3},{5,4},{6,5},{7,6},{8,7},{9,8},{10,9... | collective-permute-start | bytes 1572872 | tf_op jit(solution)/shard_map/ppermute | solution.py:17
  185.7 30.2 %collective-permute-start.6 = (f32[64,16,128]{2,0,1:T(8,128)S(1)}, f32[64,16,128]{2,0,1:T(8,128)}, u32[]{:S(2)}, u32[]{:S(2)}) collective-permute-start(f32[64,16,128]{2,0,1:T(8,128)S(1)} %broadcast_select_fusion.9), channel_id=1, source_target_pairs={{0,1},{1,2},{2,3},{3,4},{4,5},{5,6},{6,7},{7,8},{8,9},{9,10},{10,1... | collective-permute-start | bytes 1572872 | tf_op jit(solution)/shard_map/ppermute | solution.py:17
  195.1 30.9 %collective-permute-start.12 = (f32[64,16,128]{2,0,1:T(8,128)S(1)}, f32[64,16,128]{2,0,1:T(8,128)S(1)}, u32[]{:S(2)}, u32[]{:S(2)}) collective-permute-start(f32[64,16,128]{2,0,1:T(8,128)S(1)} %broadcast_select_fusion.4), channel_id=1, source_target_pairs={{0,31},{1,0},{2,1},{3,2},{4,3},{5,4},{6,5},{7,6},{8,7},{9,8},{10,9... | collective-permute-start | bytes 1572872 | tf_op jit(solution)/shard_map/ppermute | solution.py:17
  200.6 25.4 %collective-permute-start.13 = (f32[64,16,128]{2,0,1:T(8,128)S(1)}, f32[64,16,128]{2,0,1:T(8,128)}, u32[]{:S(2)}, u32[]{:S(2)}) collective-permute-start(f32[64,16,128]{2,0,1:T(8,128)S(1)} %broadcast_select_fusion.4), channel_id=1, source_target_pairs={{0,1},{1,2},{2,3},{3,4},{4,5},{5,6},{6,7},{7,8},{8,9},{9,10},{10,1... | collective-permute-start | bytes 1572872 | tf_op jit(solution)/shard_map/ppermute | solution.py:17
  246.2 1.2 copy-start.3
